TPU v7x, 32 devices: a whole 2x2x4 slice. The times are simulated.
32 devices in a mesh: energy: 16 (over z, x, core), mom: 2 (over y).
Axes of the slice: x: 2, y: 2, z: 4, core: 2. Of those that a mesh axis runs over, the one named last changes fastest.
Arguments:
- sigma_in: float32 [64, 2, 2, 256, 256], P('energy', 'mom'), may hold values from -0.1875 to 0.1875
- hamiltonian: float32 [2, 2, 256, 256], P('mom'), may hold values from -0.375 to 0.375
- coupling: float32 [2, 256, 256], P('mom'), may hold values from -0.1875 to 0.1875
- energies: float32 [64], replicated, may hold values from 1.4 to 2, as said below
- counts: int32 [64], replicated, may hold values from 2 to 4, as said below
- strengths: float32 [16], replicated, may hold values from 0.05625 to 0.1875
- offsets: int32 [16], replicated, may hold values from 0 to 1
Outputs:
- sigma_next: float32 [64, 2, 2, 256, 256], P('energy', 'mom')
Inputs may be any that keep to these rules, and one draw needn't show every extreme that they name: `energies`: increasing along the grid. `counts`: each point needs either 2 or 4 sweeps, and some point needs 4.
All inputs are finite; a program needn't handle non-finite values.
Results may differ from a plain program's by a relative error of at most 0.0003.
Values sent between devices are 32-bit elements; how exact they have to be, the bound alone decides.
A program may use at most 64 MiB of HBM per device.

v0:
```python
import jax
import jax.numpy as jnp
from jax import lax
from jax.sharding import PartitionSpec as P

PRECISE = lax.Precision.HIGHEST
MIX_RATE = 0.6
PHONON = 0.1
BROADENING = 0.02


def shifted(value, axis, steps):
    count = lax.axis_size(axis)
    pairs = [(source, (source + steps) % count) for source in range(count)]
    return lax.ppermute(value, axis, pairs)


def product(left_side, right_side):
    return jnp.dot(left_side, right_side, precision=PRECISE, preferred_element_type=jnp.float32)


def invert(matrix, energy, sweeps):
    identity = jnp.eye(matrix.shape[0], dtype=jnp.float32)

    def keep_going(carried):
        return carried[0] < sweeps

    def sweep(carried):
        estimate = carried[1]
        return (carried[0] + 1, 2.0 * estimate - product(estimate, product(matrix, estimate)))

    return lax.while_loop(keep_going, sweep, (jnp.int32(0), identity / energy))[1]


def solve_point(ham_block, coupling_block, sigma_pair, energy, sweeps):
    identity = jnp.eye(ham_block.shape[1], dtype=jnp.float32)
    left_matrix = energy * identity - ham_block[0] - sigma_pair[0]
    left_inverse = invert(left_matrix, energy, sweeps)
    inverse_coupled = product(left_inverse, coupling_block)
    coupled_inverse = product(coupling_block.T, left_inverse)
    right_matrix = (
        energy * identity
        - ham_block[1]
        - sigma_pair[1]
        - product(coupling_block.T, inverse_coupled)
    )
    right_green = invert(right_matrix, energy, sweeps)
    left_green = left_inverse + product(product(inverse_coupled, right_green), coupled_inverse)
    return jnp.stack([left_green, right_green])


def lorentz(offset):
    scaled = offset / BROADENING
    return 1.0 / (1.0 + scaled * scaled)


def build_kernel(row_energy, column_energy):
    spacing = row_energy[:, None] - column_energy[None, :]
    kernel = lorentz(spacing - PHONON) + lorentz(spacing + PHONON)
    return kernel / jnp.sum(kernel, axis=1, keepdims=True)


def body(sigma_in, hamiltonian, coupling, energies, counts, strengths, offsets):
    points = sigma_in.shape[0]
    order = sigma_in.shape[3]
    ranks = lax.axis_size("energy")
    moments = lax.axis_size("mom")
    my_rank = lax.axis_index("energy")
    own_energy = lax.dynamic_slice_in_dim(energies, my_rank * points, points)
    own_count = lax.dynamic_slice_in_dim(counts, my_rank * points, points)
    blocks = sigma_in[:, 0]

    def solve_held(held_point):
        return solve_point(hamiltonian[0], coupling[0], held_point[0], held_point[1], held_point[2])

    green_blocks = lax.map(solve_held, (blocks, own_energy, own_count))
    shift_index = jnp.arange(moments, dtype=jnp.int32)
    weights = jnp.sum(
        strengths[:, None] * (offsets[:, None] == shift_index[None, :]).astype(jnp.float32), axis=0
    )
    kernel = build_kernel(energies, energies)
    piece_width = 2 * order * order // ranks
    spread = green_blocks.reshape(points, ranks, moments, piece_width // moments)
    column = lax.all_to_all(spread, "energy", split_axis=1, concat_axis=0, tiled=True)[:, 0]
    rows_all = column.shape[0]
    flat_column = column.reshape(rows_all, -1)
    mixed_sum = weights[0] * flat_column
    for offset_step in range(1, moments):
        mixed_sum = mixed_sum + weights[offset_step] * shifted(flat_column, "mom", offset_step)
    sigma_part = product(kernel, mixed_sum).reshape(column.shape)
    result = lax.all_to_all(sigma_part[:, None], "energy", split_axis=0, concat_axis=1, tiled=True)
    sigma_new = result.reshape(sigma_in.shape)
    return (1.0 - MIX_RATE) * sigma_in + MIX_RATE * sigma_new


def solution(mesh):
    placed = (
        P("energy", "mom", None, None, None),
        P("mom", None, None, None),
        P("mom", None, None),
        P(),
        P(),
        P(),
        P(),
    )
    return jax.shard_map(
        body,
        mesh=mesh,
        in_specs=placed,
        out_specs=P("energy", "mom", None, None, None),
        check_vma=False,
    )
```

profile of v0, /device:TPU:1, one launch (start us, length us, event | category | flops | bytes accessed | tf_op | source)
XLA Modules:
  0.0 263.6 jit_solution(9605364366974160668)
XLA Ops:
  0.0 0.7 dynamic_slice.18
  0.7 0.7 dynamic_slice.19
  1.5 3.0 %copy.36 = f32[4,1,2,256,256]{3,4,2,0,1:T(8,128)} copy(f32[4,1,2,256,256]{4,3,2,1,0:T(8,128)} %param.13) | data formatting | bytes 4194304 | tf_op args[0]
  4.7 73.6 %while.32 = (s32[]{:T(128)}, f32[4,2,256,256]{3,2,1,0:T(8,128)}, f32[4]{0:T(128)S(1)}, s32[4]{0:T(128)S(1)}, f32[1,2,256,256]{2,3,1,0:T(8,128)S(1)}, /*index=5*/...) while((s32[]{:T(128)}, f32[4,2,256,256]{3,2,1,0:T(8,128)}, ...), condition=%wide.region_7.8_spmd, body=%wide.region_2.7_spmd.sunk | while | flops 1813118976 | bytes 13632415 | solution.py:76
  4.7 0.7 dynamic_slice.22
  5.4 1.7 fusion.97
  8.5 3.8 %while.33 = (s32[]{:T(128)}, f32[256,256]{0,1:T(8,128)S(1)}, s32[]{:T(128)}, f32[256,256]{1,0:T(8,128)S(1)}, s32[]{:T(128)}) while((s32[]{:T(128)}, f32[256,256]{0,1:T(8,128)S(1)}, s32[]{:T(128)}, f32[256,256]{1,0:T(8,128)S(1)}, s32[]{:T(128)}) %tuple.63), condition=%wide.region_4.4_spmd, body=%wide.region_3.3_spmd.sunk | while | flops 402784256 | bytes 2097213 | solution.py:32
  9.5 0.6 fusion.109
  11.2 0.6 fusion.109
  12.3 0.6 fusion.98
  12.9 2.2 fusion.99
  15.3 3.8 %while.34 = (s32[]{:T(128)}, f32[256,256]{0,1:T(8,128)S(1)}, s32[]{:T(128)}, f32[256,256]{1,0:T(8,128)S(1)}, s32[]{:T(128)}) while((s32[]{:T(128)}, f32[256,256]{0,1:T(8,128)S(1)}, s32[]{:T(128)}, f32[256,256]{1,0:T(8,128)S(1)}, s32[]{:T(128)}) %tuple.66), condition=%wide.region_6.6_spmd, body=%wide.region_5.5_spmd.sunk | while | flops 402784256 | bytes 2097213 | solution.py:32
  16.3 0.6 fusion.115
  18.0 0.6 fusion.115
  20.6 0.8 fusion.103
  21.5 0.6 dynamic_slice.22
  22.1 1.7 fusion.97
  25.3 3.8 %while.33 = (s32[]{:T(128)}, f32[256,256]{0,1:T(8,128)S(1)}, s32[]{:T(128)}, f32[256,256]{1,0:T(8,128)S(1)}, s32[]{:T(128)}) while((s32[]{:T(128)}, f32[256,256]{0,1:T(8,128)S(1)}, s32[]{:T(128)}, f32[256,256]{1,0:T(8,128)S(1)}, s32[]{:T(128)}) %tuple.63), condition=%wide.region_4.4_spmd, body=%wide.region_3.3_spmd.sunk | while | flops 402784256 | bytes 2097213 | solution.py:32
  26.3 0.6 fusion.109
  27.9 0.6 fusion.109
  29.1 0.6 fusion.98
  29.7 2.2 fusion.99
  32.1 3.8 %while.34 = (s32[]{:T(128)}, f32[256,256]{0,1:T(8,128)S(1)}, s32[]{:T(128)}, f32[256,256]{1,0:T(8,128)S(1)}, s32[]{:T(128)}) while((s32[]{:T(128)}, f32[256,256]{0,1:T(8,128)S(1)}, s32[]{:T(128)}, f32[256,256]{1,0:T(8,128)S(1)}, s32[]{:T(128)}) %tuple.66), condition=%wide.region_6.6_spmd, body=%wide.region_5.5_spmd.sunk | while | flops 402784256 | bytes 2097213 | solution.py:32
  33.1 0.6 fusion.115
  34.7 0.6 fusion.115
  37.4 0.8 fusion.103
  38.2 0.6 dynamic_slice.22
  38.9 1.7 fusion.97
  42.1 7.1 %while.33 = (s32[]{:T(128)}, f32[256,256]{0,1:T(8,128)S(1)}, s32[]{:T(128)}, f32[256,256]{1,0:T(8,128)S(1)}, s32[]{:T(128)}) while((s32[]{:T(128)}, f32[256,256]{0,1:T(8,128)S(1)}, s32[]{:T(128)}, f32[256,256]{1,0:T(8,128)S(1)}, s32[]{:T(128)}) %tuple.63), condition=%wide.region_4.4_spmd, body=%wide.region_3.3_spmd.sunk | while | flops 402784256 | bytes 2097213 | solution.py:32
  43.1 0.6 fusion.109
  44.7 0.6 fusion.109
  46.3 0.6 fusion.109
  48.0 0.6 fusion.109
  49.1 0.6 fusion.98
  49.7 2.2 fusion.99
  52.1 7.1 %while.34 = (s32[]{:T(128)}, f32[256,256]{0,1:T(8,128)S(1)}, s32[]{:T(128)}, f32[256,256]{1,0:T(8,128)S(1)}, s32[]{:T(128)}) while((s32[]{:T(128)}, f32[256,256]{0,1:T(8,128)S(1)}, s32[]{:T(128)}, f32[256,256]{1,0:T(8,128)S(1)}, s32[]{:T(128)}) %tuple.66), condition=%wide.region_6.6_spmd, body=%wide.region_5.5_spmd.sunk | while | flops 402784256 | bytes 2097213 | solution.py:32
  53.1 0.6 fusion.115
  54.8 0.6 fusion.115
  56.4 0.6 fusion.115
  58.0 0.6 fusion.115
  60.7 0.8 fusion.103
  61.5 0.6 dynamic_slice.22
  62.2 1.7 fusion.97
  65.3 3.8 %while.33 = (s32[]{:T(128)}, f32[256,256]{0,1:T(8,128)S(1)}, s32[]{:T(128)}, f32[256,256]{1,0:T(8,128)S(1)}, s32[]{:T(128)}) while((s32[]{:T(128)}, f32[256,256]{0,1:T(8,128)S(1)}, s32[]{:T(128)}, f32[256,256]{1,0:T(8,128)S(1)}, s32[]{:T(128)}) %tuple.63), condition=%wide.region_4.4_spmd, body=%wide.region_3.3_spmd.sunk | while | flops 402784256 | bytes 2097213 | solution.py:32
  66.4 0.6 fusion.109
  68.0 0.6 fusion.109
  69.2 0.6 fusion.98
  69.8 2.2 fusion.99
  72.1 3.8 %while.34 = (s32[]{:T(128)}, f32[256,256]{0,1:T(8,128)S(1)}, s32[]{:T(128)}, f32[256,256]{1,0:T(8,128)S(1)}, s32[]{:T(128)}) while((s32[]{:T(128)}, f32[256,256]{0,1:T(8,128)S(1)}, s32[]{:T(128)}, f32[256,256]{1,0:T(8,128)S(1)}, s32[]{:T(128)}) %tuple.66), condition=%wide.region_6.6_spmd, body=%wide.region_5.5_spmd.sunk | while | flops 402784256 | bytes 2097213 | solution.py:32
  73.2 0.6 fusion.115
  74.8 0.6 fusion.115
  77.5 0.8 fusion.103
  78.3 2.6 reshape.35
  81.2 64.2 %all_to_all.24 = f32[4,16,2,4096]{3,2,0,1:T(2,128)S(1)} all-to-all(f32[4,16,2,4096]{3,2,0,1:T(2,128)S(1)} %copy.38), channel_id=1, replica_groups=mesh['energy'=16,'mom'=2] {'energy'}, dimensions={1} | all-to-all | bytes 4194304 | tf_op jit(solution)/shard_map/all_to_all | solution.py:84
  145.4 1.2 copy.41
  146.6 1.3 collective-permute-start
  148.8 45.5 %collective-permute-done = f32[64,8192]{1,0:T(8,128)S(1)} collective-permute-done((f32[64,8192]{1,0:T(8,128)S(1)}, f32[64,8192]{1,0:T(8,128)S(1)}, u32[]{:S(2)}, u32[]{:S(2)}) %collective-permute-start) | collective-permute-done | bytes 2097184 | tf_op jit(solution)/shard_map/ppermute | solution.py:15
  194.3 3.1 %fusion.13 = f32[64,8192]{1,0:T(8,128)S(1)} fusion(f32[64,8192]{1,0:T(8,128)S(1)} %collective-permute-done, f32[64,8192]{1,0:T(8,128)S(1)} %bitcast.135, f32[]{:T(128)} %bitcast.17, f32[]{:T(128)} %bitcast.13, f32[64]{0:T(128)S(1)} %fusion.31, f32[64]{0:T(128)S(1)} %copy-done.3), kind=kOutput, calls=%fused_computation.23 | convolution fusion | flops 404279296 | bytes 6291976 | tf_op jit(solution)/shard_map/dot_general | solution.py:19
  197.5 2.8 %broadcast_in_dim_reshape.3 = f32[64,1,2,4096]{3,2,0,1:T(2,128)} reshape(f32[64,8192]{1,0:T(8,128)S(1)} %fusion.13) | data formatting | bytes 4194304 | tf_op jit(solution)/shard_map/broadcast_in_dim;reshape | solution.py:91
  200.3 52.6 %all_to_all.25 = f32[64,1,2,4096]{3,2,1,0:T(2,128)S(1)} all-to-all(f32[64,1,2,4096]{3,2,1,0:T(2,128)} %bitcast.137), channel_id=1, replica_groups=mesh['energy'=16,'mom'=2] {'energy'}, dimensions={0} | all-to-all | bytes 4194304 | tf_op jit(solution)/shard_map/all_to_all | solution.py:91
  252.8 1.9 broadcast_multiply_fusion
  254.8 1.5 copy.40
  256.2 4.2 %mul.86 = f32[4,1,2,256,256]{4,3,2,1,0:T(8,128)} reshape(f32[4,16,1,2,4096]{4,3,1,0,2:T(2,128)} %copy.40) | data formatting | bytes 4194304 | tf_op jit(solution)/shard_map/mul | solution.py:93
  260.5 3.2 %multiply_add_fusion = f32[4,1,2,256,256]{4,3,2,1,0:T(8,128)} fusion(f32[4,1,2,256,256]{4,3,2,1,0:T(8,128)} %mul.86, f32[4,1,2,256,256]{4,3,2,1,0:T(8,128)S(1)} %copy-done.1), kind=kLoop, calls=%fused_computation.27 | loop fusion | flops 1048576 | bytes 6291456 | tf_op jit(solution)/shard_map/add | solution.py:93
  (98 shorter events, 19.3 us)
Async XLA Ops:
  1.5 3.0 %copy-start.2 = (f32[1,2,256,256]{3,2,1,0:T(8,128)S(1)}, f32[1,2,256,256]{3,2,1,0:T(8,128)}, u32[]{:S(2)}) copy-start(f32[1,2,256,256]{3,2,1,0:T(8,128)} %param.14) | copy-start | bytes 1572868
  1.5 3.2 %copy-start = (f32[1,256,256]{2,1,0:T(8,128)S(1)}, f32[1,256,256]{2,1,0:T(8,128)}, u32[]{:S(2)}) copy-start(f32[1,256,256]{2,1,0:T(8,128)} %param.15) | copy-start | bytes 786436
  145.4 2.5 copy-start.4
  145.4 2.5 copy-start.5
  145.4 3.2 %copy-start.3 = (f32[64]{0:T(128)S(1)}, f32[64]{0:T(128)}, u32[]{:S(2)}) copy-start(f32[64]{0:T(128)} %param.16) | copy-start | bytes 772
  146.6 47.7 %collective-permute-start = (f32[64,8192]{1,0:T(8,128)S(1)}, f32[64,8192]{1,0:T(8,128)S(1)}, u32[]{:S(2)}, u32[]{:S(2)}) collective-permute-start(f32[64,8192]{1,0:T(8,128)S(1)} %bitcast.134), channel_id=1, source_target_pairs={{0,1},{1,0},{2,3},{3,2},{4,5},{5,4},{6,7},{7,6},{8,9},{9,8},{10,11... | collective-permute-start | bytes 6291464 | tf_op jit(solution)/shard_map/ppermute | solution.py:15
  256.2 4.2 %copy-start.1 = (f32[4,1,2,256,256]{4,3,2,1,0:T(8,128)S(1)}, f32[4,1,2,256,256]{4,3,2,1,0:T(8,128)}, u32[]{:S(2)}) copy-start(f32[4,1,2,256,256]{4,3,2,1,0:T(8,128)} %param.13) | copy-start | bytes 6291460
where the time goes:
time: 265 us; the launch traced here: 264 us
  blocking collectives  117 us (44%)
  waiting for transfers between devices  45.5 us (17%)
  matrix products  39.5 us (15%)
  local copies, waits for them, and re-layouts  25.2 us (10%)
  loops' own time  19.8 us (7%)
  other arithmetic  15.5 us (6%)
    all_to_all x1, blocking collectives, body(): lax.all_to_all(spread, 'energy', split_axis=1, concat_axis=0, tiled=True)  64.2 us
    all_to_all x1, blocking collectives, body(): lax.all_to_all(sigma_part[:, None], 'energy', split_axis=0, concat_axis=1...  52.6 us
    ppermute x1, waiting for transfers between devices, shifted(): return lax.ppermute(value, axis, pairs)  45.5 us
    dot_general x61, matrix products, product(): jnp.dot(left_side, right_side, precision=PRECISE, preferred_element_type=...  39.5 us
    another operation x8, loops' own time, invert(): lax.while_loop(keep_going, sweep, (jnp.int32(0), identity / energy))[1]  16.5 us
    sub x4, other arithmetic, solve_point(): left_matrix = energy * identity - ham_block[0] - sigma_pair[0]  6.66 us
    mul x2, local copies, waits for them, and re-layouts, body(): return (1.0 - MIX_RATE) * sigma_in + MIX_RATE * sigma_new  5.67 us
  transfers between devices with their start and end apart: 1, of which 1 were waited for; matrix products, arithmetic and copies ran while one was open for 0% of the time, Pallas kernels for 0%

commit v1 on v0

--- a/solution.py
+++ b/solution.py
@@ -81,7 +81,12 @@
     kernel = build_kernel(energies, energies)
     piece_width = 2 * order * order // ranks
     spread = green_blocks.reshape(points, ranks, moments, piece_width // moments)
-    column = lax.all_to_all(spread, "energy", split_axis=1, concat_axis=0, tiled=True)[:, 0]
+    column = jnp.concatenate(
+        lax.all_to_all(
+            jnp.stack(jnp.split(spread, lax.axis_size("energy"), axis=1)), "energy", 0, 0
+        ),
+        axis=0,
+    )[:, 0]
     rows_all = column.shape[0]
     flat_column = column.reshape(rows_all, -1)
     mixed_sum = weights[0] * flat_column

time: 265 us -> 265 us (level)
  no operation moved by 1% of the time
where the time goes in v1:
time: 265 us; the launch traced here: 264 us
  blocking collectives  117 us (44%)
  waiting for transfers between devices  45.5 us (17%)
  matrix products  39.5 us (15%)
  local copies, waits for them, and re-layouts  25.3 us (10%)
  loops' own time  19.8 us (7%)
  other arithmetic  15.5 us (6%)
    all_to_all x1, blocking collectives, body(): lax.all_to_all(jnp.stack(jnp.split(spread, lax.axis_size('energy'), axis=...  64.2 us
    all_to_all x1, blocking collectives, body(): lax.all_to_all(sigma_part[:, None], 'energy', split_axis=0, concat_axis=1...  52.6 us
    ppermute x1, waiting for transfers between devices, shifted(): return lax.ppermute(value, axis, pairs)  45.5 us
    dot_general x61, matrix products, product(): jnp.dot(left_side, right_side, precision=PRECISE, preferred_element_type=...  39.5 us
    another operation x8, loops' own time, invert(): lax.while_loop(keep_going, sweep, (jnp.int32(0), identity / energy))[1]  16.5 us
    sub x4, other arithmetic, solve_point(): left_matrix = energy * identity - ham_block[0] - sigma_pair[0]  6.66 us
    mul x2, local copies, waits for them, and re-layouts, body(): return (1.0 - MIX_RATE) * sigma_in + MIX_RATE * sigma_new  5.67 us
  transfers between devices with their start and end apart: 1, of which 1 were waited for; matrix products, arithmetic and copies ran while one was open for 0% of the time, Pallas kernels for 0%

profile of v1, /device:TPU:1, one launch (start us, length us, event | category | flops | bytes accessed | tf_op | source)
XLA Modules:
  0.0 263.8 jit_solution(6706498523941754992)
XLA Ops:
  0.0 0.7 dynamic_slice.18
  0.7 0.7 dynamic_slice.19
  1.5 3.0 %copy.57 = f32[4,1,2,256,256]{3,4,2,0,1:T(8,128)} copy(f32[4,1,2,256,256]{4,3,2,1,0:T(8,128)} %param.13) | data formatting | bytes 4194304 | tf_op args[0]
  4.7 73.6 %while.32 = (s32[]{:T(128)}, f32[4,2,256,256]{3,2,1,0:T(8,128)}, f32[4]{0:T(128)S(1)}, s32[4]{0:T(128)S(1)}, f32[1,2,256,256]{2,3,1,0:T(8,128)S(1)}, /*index=5*/...) while((s32[]{:T(128)}, f32[4,2,256,256]{3,2,1,0:T(8,128)}, ...), condition=%wide.region_7.8_spmd, body=%wide.region_2.7_spmd.sunk | while | flops 1813118976 | bytes 13632415 | solution.py:76
  4.7 0.7 dynamic_slice.22
  5.4 1.7 fusion.113
  8.5 3.8 %while.33 = (s32[]{:T(128)}, f32[256,256]{0,1:T(8,128)S(1)}, s32[]{:T(128)}, f32[256,256]{1,0:T(8,128)S(1)}, s32[]{:T(128)}) while((s32[]{:T(128)}, f32[256,256]{0,1:T(8,128)S(1)}, s32[]{:T(128)}, f32[256,256]{1,0:T(8,128)S(1)}, s32[]{:T(128)}) %tuple.60), condition=%wide.region_4.4_spmd, body=%wide.region_3.3_spmd.sunk | while | flops 402784256 | bytes 2097213 | solution.py:32
  9.5 0.6 fusion.125
  11.2 0.6 fusion.125
  12.3 0.6 fusion.114
  12.9 2.2 fusion.115
  15.3 3.8 %while.34 = (s32[]{:T(128)}, f32[256,256]{0,1:T(8,128)S(1)}, s32[]{:T(128)}, f32[256,256]{1,0:T(8,128)S(1)}, s32[]{:T(128)}) while((s32[]{:T(128)}, f32[256,256]{0,1:T(8,128)S(1)}, s32[]{:T(128)}, f32[256,256]{1,0:T(8,128)S(1)}, s32[]{:T(128)}) %tuple.63), condition=%wide.region_6.6_spmd, body=%wide.region_5.5_spmd.sunk | while | flops 402784256 | bytes 2097213 | solution.py:32
  16.3 0.6 fusion.131
  18.0 0.6 fusion.131
  20.6 0.8 fusion.119
  21.5 0.6 dynamic_slice.22
  22.1 1.7 fusion.113
  25.3 3.8 %while.33 = (s32[]{:T(128)}, f32[256,256]{0,1:T(8,128)S(1)}, s32[]{:T(128)}, f32[256,256]{1,0:T(8,128)S(1)}, s32[]{:T(128)}) while((s32[]{:T(128)}, f32[256,256]{0,1:T(8,128)S(1)}, s32[]{:T(128)}, f32[256,256]{1,0:T(8,128)S(1)}, s32[]{:T(128)}) %tuple.60), condition=%wide.region_4.4_spmd, body=%wide.region_3.3_spmd.sunk | while | flops 402784256 | bytes 2097213 | solution.py:32
  26.3 0.6 fusion.125
  27.9 0.6 fusion.125
  29.1 0.6 fusion.114
  29.7 2.2 fusion.115
  32.1 3.8 %while.34 = (s32[]{:T(128)}, f32[256,256]{0,1:T(8,128)S(1)}, s32[]{:T(128)}, f32[256,256]{1,0:T(8,128)S(1)}, s32[]{:T(128)}) while((s32[]{:T(128)}, f32[256,256]{0,1:T(8,128)S(1)}, s32[]{:T(128)}, f32[256,256]{1,0:T(8,128)S(1)}, s32[]{:T(128)}) %tuple.63), condition=%wide.region_6.6_spmd, body=%wide.region_5.5_spmd.sunk | while | flops 402784256 | bytes 2097213 | solution.py:32
  33.1 0.6 fusion.131
  34.7 0.6 fusion.131
  37.4 0.8 fusion.119
  38.2 0.6 dynamic_slice.22
  38.9 1.7 fusion.113
  42.1 7.1 %while.33 = (s32[]{:T(128)}, f32[256,256]{0,1:T(8,128)S(1)}, s32[]{:T(128)}, f32[256,256]{1,0:T(8,128)S(1)}, s32[]{:T(128)}) while((s32[]{:T(128)}, f32[256,256]{0,1:T(8,128)S(1)}, s32[]{:T(128)}, f32[256,256]{1,0:T(8,128)S(1)}, s32[]{:T(128)}) %tuple.60), condition=%wide.region_4.4_spmd, body=%wide.region_3.3_spmd.sunk | while | flops 402784256 | bytes 2097213 | solution.py:32
  43.1 0.6 fusion.125
  44.7 0.6 fusion.125
  46.3 0.6 fusion.125
  48.0 0.6 fusion.125
  49.1 0.6 fusion.114
  49.7 2.2 fusion.115
  52.1 7.1 %while.34 = (s32[]{:T(128)}, f32[256,256]{0,1:T(8,128)S(1)}, s32[]{:T(128)}, f32[256,256]{1,0:T(8,128)S(1)}, s32[]{:T(128)}) while((s32[]{:T(128)}, f32[256,256]{0,1:T(8,128)S(1)}, s32[]{:T(128)}, f32[256,256]{1,0:T(8,128)S(1)}, s32[]{:T(128)}) %tuple.63), condition=%wide.region_6.6_spmd, body=%wide.region_5.5_spmd.sunk | while | flops 402784256 | bytes 2097213 | solution.py:32
  53.1 0.6 fusion.131
  54.8 0.6 fusion.131
  56.4 0.6 fusion.131
  58.0 0.6 fusion.131
  60.7 0.8 fusion.119
  61.5 0.6 dynamic_slice.22
  62.2 1.7 fusion.113
  65.3 3.8 %while.33 = (s32[]{:T(128)}, f32[256,256]{0,1:T(8,128)S(1)}, s32[]{:T(128)}, f32[256,256]{1,0:T(8,128)S(1)}, s32[]{:T(128)}) while((s32[]{:T(128)}, f32[256,256]{0,1:T(8,128)S(1)}, s32[]{:T(128)}, f32[256,256]{1,0:T(8,128)S(1)}, s32[]{:T(128)}) %tuple.60), condition=%wide.region_4.4_spmd, body=%wide.region_3.3_spmd.sunk | while | flops 402784256 | bytes 2097213 | solution.py:32
  66.4 0.6 fusion.125
  68.0 0.6 fusion.125
  69.2 0.6 fusion.114
  69.8 2.2 fusion.115
  72.1 3.8 %while.34 = (s32[]{:T(128)}, f32[256,256]{0,1:T(8,128)S(1)}, s32[]{:T(128)}, f32[256,256]{1,0:T(8,128)S(1)}, s32[]{:T(128)}) while((s32[]{:T(128)}, f32[256,256]{0,1:T(8,128)S(1)}, s32[]{:T(128)}, f32[256,256]{1,0:T(8,128)S(1)}, s32[]{:T(128)}) %tuple.63), condition=%wide.region_6.6_spmd, body=%wide.region_5.5_spmd.sunk | while | flops 402784256 | bytes 2097213 | solution.py:32
  73.2 0.6 fusion.131
  74.8 0.6 fusion.131
  77.5 0.8 fusion.119
  78.3 2.6 reshape.34
  81.4 64.2 %all_to_all.14 = f32[16,4,1,2,4096]{4,3,1,2,0:T(2,128)S(1)} all-to-all(f32[16,4,1,2,4096]{4,3,1,2,0:T(2,128)S(1)} %fusion.19), channel_id=1, replica_groups=mesh['energy'=16,'mom'=2] {'energy'}, dimensions={0} | all-to-all | bytes 4194304 | tf_op jit(solution)/shard_map/all_to_all | solution.py:85
  145.6 1.2 copy.91
  146.8 1.3 collective-permute-start
  149.0 45.5 %collective-permute-done = f32[64,8192]{1,0:T(8,128)S(1)} collective-permute-done((f32[64,8192]{1,0:T(8,128)S(1)}, f32[64,8192]{1,0:T(8,128)S(1)}, u32[]{:S(2)}, u32[]{:S(2)}) %collective-permute-start) | collective-permute-done | bytes 2097184 | tf_op jit(solution)/shard_map/ppermute | solution.py:15
  194.5 3.2 %fusion.13 = f32[64,8192]{1,0:T(8,128)S(1)} fusion(f32[64,8192]{1,0:T(8,128)S(1)} %collective-permute-done, f32[64,8192]{1,0:T(8,128)S(1)} %bitcast.226, f32[]{:T(128)} %bitcast.31, f32[]{:T(128)} %bitcast.13, f32[64]{0:T(128)S(1)} %fusion.47, f32[64]{0:T(128)S(1)} %copy-done.3), kind=kOutput, calls=%fused_computation.23 | convolution fusion | flops 404279296 | bytes 6291976 | tf_op jit(solution)/shard_map/dot_general | solution.py:19
  197.7 2.8 %broadcast_in_dim_reshape.3 = f32[64,1,2,4096]{3,2,0,1:T(2,128)} reshape(f32[64,8192]{1,0:T(8,128)S(1)} %fusion.13) | data formatting | bytes 4194304 | tf_op jit(solution)/shard_map/broadcast_in_dim;reshape | solution.py:96
  200.5 52.6 %all_to_all.15 = f32[64,1,2,4096]{3,2,1,0:T(2,128)S(1)} all-to-all(f32[64,1,2,4096]{3,2,1,0:T(2,128)} %bitcast.228), channel_id=1, replica_groups=mesh['energy'=16,'mom'=2] {'energy'}, dimensions={0} | all-to-all | bytes 4194304 | tf_op jit(solution)/shard_map/all_to_all | solution.py:96
  253.0 1.9 broadcast_multiply_fusion
  255.0 1.5 copy.75
  256.4 4.2 %mul.86 = f32[4,1,2,256,256]{4,3,2,1,0:T(8,128)} reshape(f32[4,16,1,2,4096]{4,3,1,0,2:T(2,128)} %copy.75) | data formatting | bytes 4194304 | tf_op jit(solution)/shard_map/mul | solution.py:98
  260.6 3.2 %multiply_add_fusion = f32[4,1,2,256,256]{4,3,2,1,0:T(8,128)} fusion(f32[4,1,2,256,256]{4,3,2,1,0:T(8,128)} %mul.86, f32[4,1,2,256,256]{4,3,2,1,0:T(8,128)S(1)} %copy-done.1), kind=kLoop, calls=%fused_computation.27 | loop fusion | flops 1048576 | bytes 6291456 | tf_op jit(solution)/shard_map/add | solution.py:98
  (113 shorter events, 19.4 us)
Async XLA Ops:
  1.5 3.0 %copy-start.2 = (f32[1,2,256,256]{3,2,1,0:T(8,128)S(1)}, f32[1,2,256,256]{3,2,1,0:T(8,128)}, u32[]{:S(2)}) copy-start(f32[1,2,256,256]{3,2,1,0:T(8,128)} %param.14) | copy-start | bytes 1572868
  1.5 3.2 %copy-start = (f32[1,256,256]{2,1,0:T(8,128)S(1)}, f32[1,256,256]{2,1,0:T(8,128)}, u32[]{:S(2)}) copy-start(f32[1,256,256]{2,1,0:T(8,128)} %param.15) | copy-start | bytes 786436
  145.6 2.5 copy-start.4
  145.6 2.5 copy-start.5
  145.6 3.2 %copy-start.3 = (f32[64]{0:T(128)S(1)}, f32[64]{0:T(128)}, u32[]{:S(2)}) copy-start(f32[64]{0:T(128)} %param.16) | copy-start | bytes 772
  146.8 47.7 %collective-permute-start = (f32[64,8192]{1,0:T(8,128)S(1)}, f32[64,8192]{1,0:T(8,128)S(1)}, u32[]{:S(2)}, u32[]{:S(2)}) collective-permute-start(f32[64,8192]{1,0:T(8,128)S(1)} %bitcast.225), channel_id=1, source_target_pairs={{0,1},{1,0},{2,3},{3,2},{4,5},{5,4},{6,7},{7,6},{8,9},{9,8},{10,11... | collective-permute-start | bytes 6291464 | tf_op jit(solution)/shard_map/ppermute | solution.py:15
  256.4 4.2 %copy-start.1 = (f32[4,1,2,256,256]{4,3,2,1,0:T(8,128)S(1)}, f32[4,1,2,256,256]{4,3,2,1,0:T(8,128)}, u32[]{:S(2)}) copy-start(f32[4,1,2,256,256]{4,3,2,1,0:T(8,128)} %param.13) | copy-start | bytes 6291460
